TPU v7x, 32 devices: a whole 2x2x4 slice. The times are simulated.
32 devices in a mesh: ctx: 8 (over z, y), head: 4 (over x, core).
Axes of the slice: x: 2, y: 2, z: 4, core: 2. Of those that a mesh axis runs over, the one named last changes fastest.
Arguments:
- query_rows: bfloat16 [1024, 4096], P('ctx', 'head'), may hold values from -0.3125 to 0.3125
- key_rows: bfloat16 [1024, 4096], P('ctx', 'head'), may hold values from -0.3125 to 0.3125
- value_rows: bfloat16 [1024, 4096], P('ctx', 'head'), may hold values from -0.3125 to 0.3125
- out_grad: bfloat16 [1024, 4096], P('ctx', 'head'), may hold values from -6 to 6
Outputs:
- grad_query: float32 [1024, 4096], P('ctx', 'head')
- grad_key: float32 [1024, 4096], P('ctx', 'head')
- grad_value: float32 [1024, 4096], P('ctx', 'head')
All inputs are finite; a program needn't handle non-finite values.
Results may differ from a plain program's by a relative error of at most 0.0029.
Values sent between devices are 32-bit elements; how exact they have to be, the bound alone decides.
A program may use at most 128 MiB of HBM per device.

v0:
```python
import jax
import jax.numpy as jnp
from jax import lax
from jax.sharding import PartitionSpec as P

DH = 128


def carried_in(x, axis, combine, identity, reverse):
    size, mine = (lax.axis_size(axis), lax.axis_index(axis))
    everything = lax.all_gather(x, axis)
    start = jnp.broadcast_to(jnp.asarray(identity, x.dtype), x.shape)

    def step(k, before):
        at = size - 1 - k if reverse else k
        reached = at > mine if reverse else at < mine
        new = combine(before, everything[at])
        return jnp.where(reached, new, before)

    return lax.fori_loop(0, size, step, start)


def add_states(earlier, later):
    return earlier + later


def per_device(query_rows, key_rows, value_rows, out_grad):
    tok_rows = query_rows.shape[0]
    feature_width = query_rows.shape[1]
    local_heads = feature_width // DH
    query_pieces = query_rows.reshape(tok_rows, local_heads, DH)
    key_pieces = key_rows.reshape(tok_rows, local_heads, DH)
    value_pieces = value_rows.reshape(tok_rows, local_heads, DH)
    gradient_pieces = out_grad.reshape(tok_rows, local_heads, DH)
    single_float = jnp.float32
    local_state = jnp.einsum(
        "ric,rij->icj", key_pieces, value_pieces, preferred_element_type=single_float
    )
    local_gradient = jnp.einsum(
        "ric,rij->icj", query_pieces, gradient_pieces, preferred_element_type=single_float
    )
    zeros_init = jnp.zeros_like(local_state)
    prefix = carried_in(local_state, "ctx", add_states, zeros_init, False)
    suffix = carried_in(local_gradient, "ctx", add_states, zeros_init, True)
    leading_half = prefix.astype(jnp.bfloat16)
    trailing_half = suffix.astype(jnp.bfloat16)
    positions = lax.broadcasted_iota(jnp.int32, (tok_rows, tok_rows), 0)
    sources = lax.broadcasted_iota(jnp.int32, (tok_rows, tok_rows), 1)
    causal = (positions >= sources)[None]
    score_matrix = jnp.einsum(
        "thk,shk->hts", query_pieces, key_pieces, preferred_element_type=single_float
    )
    score_matrix = jnp.where(causal, score_matrix, 0.0).astype(jnp.bfloat16)
    score_gradient = jnp.einsum(
        "thv,shv->hts", gradient_pieces, value_pieces, preferred_element_type=single_float
    )
    score_gradient = jnp.where(causal, score_gradient, 0.0).astype(jnp.bfloat16)
    grad_query = jnp.einsum(
        "duq,qdg->udg", score_gradient, key_pieces, preferred_element_type=single_float
    )
    grad_query = grad_query + jnp.einsum(
        "yfe,foe->yfo", gradient_pieces, leading_half, preferred_element_type=single_float
    )
    grad_key = jnp.einsum(
        "wlf,lwa->fwa", score_gradient, query_pieces, preferred_element_type=single_float
    )
    grad_key = grad_key + jnp.einsum(
        "fdw,duw->fdu", value_pieces, trailing_half, preferred_element_type=single_float
    )
    grad_value = jnp.einsum(
        "ulq,lug->qug", score_matrix, gradient_pieces, preferred_element_type=single_float
    )
    grad_value = grad_value + jnp.einsum(
        "zga,gau->zgu", key_pieces, trailing_half, preferred_element_type=single_float
    )
    return (
        grad_query.reshape(tok_rows, feature_width),
        grad_key.reshape(tok_rows, feature_width),
        grad_value.reshape(tok_rows, feature_width),
    )


def solution(mesh):
    in_specs = (P("ctx", "head"), P("ctx", "head"), P("ctx", "head"), P("ctx", "head"))
    out_specs = (P("ctx", "head"), P("ctx", "head"), P("ctx", "head"))
    return jax.shard_map(
        per_device, mesh=mesh, in_specs=in_specs, out_specs=out_specs, check_vma=False
    )
```

profile of v0, /device:TPU:0, one launch (start us, length us, event | category | flops | bytes accessed | tf_op | source)
XLA Modules:
  0.0 180.8 jit_solution(12506145891288632089)
XLA Ops:
  8.1 2.0 %fusion.12 = f32[8,128,128]{2,1,0:T(8,128)} fusion(bf16[128,1024]{1,0:T(8,128)(2,1)S(1)} %copy-done, bf16[128,1024]{1,0:T(8,128)(2,1)} %param.10), kind=kOutput, calls=%fused_computation.20 | convolution fusion | flops 33554432 | bytes 1048576 | tf_op jit(solution)/shard_map/ric,rij->icj/dot_general | solution.py:36
  10.2 1.1 copy.41
  11.3 2.1 %fusion.5 = f32[8,128,128]{2,1,0:T(8,128)} fusion(bf16[128,8,128]{0,2,1:T(8,128)(2,1)S(1)} %bitcast.98, bf16[128,1024]{1,0:T(8,128)(2,1)} %param.8), kind=kOutput, calls=%fused_computation.15 | convolution fusion | flops 33554432 | bytes 1048576 | tf_op jit(solution)/shard_map/ric,rij->icj/dot_general | solution.py:39
  13.5 1.3 fusion.3
  15.5 71.3 %all-gather.5.cloned.1.call-done = f32[64,128,128]{2,1,0:T(8,128)} async-done(((f32[8,128,128]{2,1,0:T(8,128)}), f32[64,128,128]{2,1,0:T(8,128)}) %all-gather.5.cloned.1.call-update) | async-done | bytes 4194320 | tf_op jit(solution)/shard_map/all_gather | solution.py:11
  86.9 10.0 %while.30 = (s32[]{:T(128)}, f32[8,128,128]{2,1,0:T(8,128)S(1)}, s32[]{:T(128)}, f32[8,8,128,128]{3,2,1,0:T(8,128)}, s32[]{:T(128)}, /*index=5*/s32[]{:T(128)}) while((s32[]{:T(128)}, f32[8,128,128]{2,1,0:T(8,128)S(1)}, s32[]{:T(128)}, f32[8,8,128,128]{3,2,1,0:T(8,128)}, s32[]{:T(128)}, /*index=5*/s32[]{:T(128)}) %tuple.84), condition=%wide.region_1.2_spmd.clone, body=%wide.region_0.1_spmd.clone.sunk | while | flops 393220 | bytes 1572965 | solution.py:20
  86.9 1.2 add_select_fusion.4
  88.1 1.2 add_select_fusion.4
  89.4 1.2 add_select_fusion.4
  90.6 1.2 add_select_fusion.4
  91.9 1.2 add_select_fusion.4
  93.1 1.2 add_select_fusion.4
  94.4 1.3 add_select_fusion.4
  95.7 1.2 add_select_fusion.4
  98.5 62.8 %all-gather.7.cloned.1.call-done = f32[64,128,128]{2,1,0:T(8,128)} async-done(((f32[8,128,128]{2,1,0:T(8,128)}), f32[64,128,128]{2,1,0:T(8,128)}) %all-gather.7.cloned.1.call-update) | async-done | bytes 4194320 | tf_op jit(solution)/shard_map/all_gather | solution.py:11
  161.3 10.0 %while.31 = (s32[]{:T(128)}, f32[8,128,128]{2,1,0:T(8,128)S(1)}, s32[]{:T(128)}, f32[8,8,128,128]{3,2,1,0:T(8,128)}, s32[]{:T(128)}, /*index=5*/s32[]{:T(128)}, s32[]{:T(128)}, s32[]{:T(128)}) while((s32[]{:T(128)}, f32[8,128,128]{2,1,0:T(8,128)S(1)}, s32[]{:T(128)}, f32[8,8,128,128]{3,2,1,0:T(8,128)}, s32[]{:T(128)}, ...), condition=%wide.region_3.4_spmd.clone, body=%wide.region_2.3_spmd.clone.sunk | while | flops 393224 | bytes 1573027 | solution.py:20
  161.3 1.2 add_select_fusion.5
  162.5 1.2 add_select_fusion.5
  163.8 1.2 add_select_fusion.5
  165.0 1.2 add_select_fusion.5
  166.3 1.2 add_select_fusion.5
  167.5 1.2 add_select_fusion.5
  168.8 1.2 add_select_fusion.5
  170.0 1.2 add_select_fusion.5
  (22 shorter events, 6.0 us)
Async XLA Ops:
  7.2 1.0 copy-start
  7.2 7.6 %copy-start.1 = (bf16[128,1024]{1,0:T(8,128)(2,1)S(1)}, bf16[128,1024]{1,0:T(8,128)(2,1)}, u32[]{:S(2)}) copy-start(bf16[128,1024]{1,0:T(8,128)(2,1)} %param.8) | copy-start | bytes 786436
  7.2 79.7 %all-gather.5.cloned.1.call-start = ((), (), s32[]{:S(2)}) async-start(), calls=%async_computation | async-start | bytes 4718592 | tf_op jit(solution)/shard_map/all_gather | solution.py:11
  10.2 151.1 %all-gather.7.cloned.1.call-start = ((), (), s32[]{:S(2)}) async-start(), calls=%async_computation.1 | async-start | bytes 4718592 | tf_op jit(solution)/shard_map/all_gather | solution.py:11
  98.5 72.8 %copy-start.2 = (bf16[128,1024]{1,0:T(8,128)(2,1)S(1)}, bf16[128,1024]{1,0:T(8,128)(2,1)}, u32[]{:S(2)}) copy-start(bf16[128,1024]{1,0:T(8,128)(2,1)} %param.10) | copy-start | bytes 786436
Sparse Core Ops, SparseCore 0:
  10.7 76.0 all-gather.4
  89.6 71.6 all-gather.6
where the time goes:
time: 182 us; the launch traced here: 181 us
  waiting for transfers between devices  134 us (74%)
  other arithmetic  19.7 us (11%)
  between operations  14.1 us (8%)
  matrix products  7.32 us (4%)
  local copies, waits for them, and re-layouts  5.02 us (3%)
    all_gather x2, waiting for transfers between devices, carried_in(): everything = lax.all_gather(x, axis)  134 us
    select_n x16, other arithmetic, step(): return jnp.where(reached, new, before)  19.7 us
    unnamed x9, local copies, waits for them, and re-layouts  3.9 us
  transfers between devices with their start and end apart: 2, of which 2 were waited for; matrix products, arithmetic and copies ran while one was open for 9% of the time, Pallas kernels for 0%

commit v1 on v0

v1 whole, which is shorter than its diff:
```python
import functools

import jax
import jax.numpy as jnp
from jax import lax
from jax.experimental import pallas as pl
from jax.experimental.pallas import tpu as pltpu
from jax.sharding import PartitionSpec as P

DH = 128
MESH = pl.DeviceIdType.MESH
F32 = jnp.float32
BF16 = jnp.bfloat16


def dot(left, right, over_left, over_right):
    return lax.dot_general(
        left, right, (((over_left,), (over_right,)), ((), ())), preferred_element_type=F32
    )


def kernel(
    n, heads,
    q_hbm, k_hbm, v_hbm, g_hbm, dq_hbm, dk_hbm, dv_hbm,
    rows, own, partner, carry_in, carry_out, grads,
    load_sem, store_sem, swap_send, swap_recv, chain_send, chain_recv,
):
    tok = rows.shape[1]
    me = lax.axis_index("ctx")
    side = lax.rem(me, 2)
    row = me // 2
    last = n // 2 - 1
    other = me + 1 - 2 * side

    loads = [
        pltpu.make_async_copy(src, rows.at[i], load_sem.at[i])
        for i, src in enumerate((k_hbm, v_hbm, q_hbm, g_hbm))
    ]
    for load in loads:
        load.start()

    barrier = pltpu.get_barrier_semaphore()

    def greet(device):
        pl.semaphore_signal(barrier, inc=1, device_id={"ctx": device}, device_id_type=MESH)

    greet(other)

    @pl.when(row > 0)
    def _():
        greet(me - 2)

    @pl.when(row < last)
    def _():
        greet(me + 2)

    peers = 1 + jnp.where(row > 0, 1, 0) + jnp.where(row < last, 1, 0)
    pl.semaphore_wait(barrier, peers)

    for load in loads:
        load.wait()

    def swap(kind, h):
        return pltpu.make_async_remote_copy(
            src_ref=own.at[kind, h],
            dst_ref=partner.at[kind, h],
            send_sem=swap_send.at[kind, h],
            recv_sem=swap_recv.at[kind, h],
            device_id={"ctx": other},
            device_id_type=MESH,
        )

    def chain(kind, h):
        return pltpu.make_async_remote_copy(
            src_ref=carry_out.at[kind, h],
            dst_ref=carry_in.at[kind, h],
            send_sem=chain_send.at[kind, h],
            recv_sem=chain_recv.at[kind, h],
            device_id={"ctx": me + 2 - 4 * kind},
            device_id_type=MESH,
        )

    def columns(h):
        return pl.ds(pl.multiple_of(h * DH, DH), DH)

    early = jnp.where(2 * row <= last, 0, 1)

    def edge(kind):
        return jnp.where(kind == 0, last, 0)

    def begin(kind):
        return jnp.where(kind == 0, 0, last)

    def start_swaps(kind):
        needed = (row != edge(kind)) | (side == kind)

        def one(h, _):
            own[kind, h] = dot(rows[2 * kind, :, columns(h)], rows[2 * kind + 1, :, columns(h)], 0, 0)

            @pl.when(needed)
            def _():
                swap(kind, h).start()

            return 0

        lax.fori_loop(0, heads, one, 0)

    def store(i, h):
        out = (dq_hbm, dk_hbm, dv_hbm)[i]
        return pltpu.make_async_copy(
            grads.at[i, :, columns(h)], out.at[:, columns(h)], store_sem.at[i, h]
        )

    def carry(kind, h):
        takes = (row != edge(kind)) | (side == 1 - kind)

        @pl.when(takes)
        def _():
            swap(kind, h).wait_recv()

        @pl.when(row != begin(kind))
        def _():
            chain(kind, h).wait_recv()

        before = jnp.where(row != begin(kind), carry_in[kind, h], 0.0)

        @pl.when(row != edge(kind))
        def _():
            carry_out[kind, h] = before + own[kind, h] + partner[kind, h]
            chain(kind, h).start()

        total = before + jnp.where(side == 1 - kind, partner[kind, h], 0.0)
        total = total.astype(BF16)

        @pl.when(kind == 0)
        def _():
            grads[0, :, columns(h)] += dot(rows[3, :, columns(h)], total, 1, 1)
            store(0, h).start()

        @pl.when(kind == 1)
        def _():
            grads[1, :, columns(h)] += dot(rows[1, :, columns(h)], total, 1, 1)
            store(1, h).start()
            grads[2, :, columns(h)] += dot(rows[0, :, columns(h)], total, 1, 0)
            store(2, h).start()

    start_swaps(early)
    start_swaps(1 - early)

    down = lax.broadcasted_iota(jnp.int32, (tok, tok), 0)
    across = lax.broadcasted_iota(jnp.int32, (tok, tok), 1)

    def first(h, _):
        k, v, q, g = (rows[i, :, columns(h)] for i in range(4))
        dprob = jnp.where(down >= across, dot(g, v, 1, 1), 0.0).astype(BF16)
        dprob_t = jnp.where(down <= across, dot(v, g, 1, 1), 0.0).astype(BF16)
        scores_t = jnp.where(down <= across, dot(k, q, 1, 1), 0.0).astype(BF16)
        grads[0, :, columns(h)] = dot(dprob, k, 1, 0)
        grads[1, :, columns(h)] = dot(dprob_t, q, 1, 0)
        grads[2, :, columns(h)] = dot(scores_t, g, 1, 0)
        carry(early, h)
        return 0

    lax.fori_loop(0, heads, first, 0)

    def second(h, _):
        carry(1 - early, h)
        return 0

    lax.fori_loop(0, heads, second, 0)

    def drain(h, _):
        for kind in range(2):
            @pl.when((row != edge(kind)) | (side == kind))
            def _():
                swap(kind, h).wait_send()

            @pl.when(row != edge(kind))
            def _():
                chain(kind, h).wait_send()

        for i in range(3):
            store(i, h).wait()
        return 0

    lax.fori_loop(0, heads, drain, 0)


def solution(mesh):
    n = mesh.shape["ctx"]

    def per_device(query_rows, key_rows, value_rows, out_grad):
        tok, width = query_rows.shape
        heads = width // DH
        states = pltpu.VMEM((2, heads, DH, DH), F32)
        sems = pltpu.SemaphoreType.DMA((2, heads))
        return pl.pallas_call(
            functools.partial(kernel, n, heads),
            out_shape=[jax.ShapeDtypeStruct((tok, width), F32)] * 3,
            in_specs=[pl.BlockSpec(memory_space=pl.ANY)] * 4,
            out_specs=[pl.BlockSpec(memory_space=pl.ANY)] * 3,
            scratch_shapes=[
                pltpu.VMEM((4, tok, width), BF16),
                states, states, states, states,
                pltpu.VMEM((3, tok, width), F32),
                pltpu.SemaphoreType.DMA((4,)),
                pltpu.SemaphoreType.DMA((3, heads)),
                sems, sems, sems, sems,
            ],
            compiler_params=pltpu.CompilerParams(
                collective_id=0, has_side_effects=True, vmem_limit_bytes=32 << 20
            ),
        )(query_rows, key_rows, value_rows, out_grad)

    spec = P("ctx", "head")
    return jax.shard_map(
        per_device, mesh=mesh, in_specs=(spec,) * 4, out_specs=(spec,) * 3, check_vma=False
    )
```

time: 182 us -> 40.9 us (0.22)
  waiting for transfers between devices: 134 us -> 0 us
  Pallas kernels: 0 us -> 33.9 us
  other arithmetic: 19.7 us -> 0 us
  between operations: 14.1 us -> 0.65 us
  matrix products: 7.32 us -> 0 us
    all_gather x2 -> x0, waiting for transfers between devices: 134 us -> none  [carried_in(): everything = lax.all_gather(x, axis)]
    pallas_call x0 -> x1, Pallas kernels: none -> 33.9 us  [per_device(): pl.pallas_call(functools.partial(kernel, n, heads), out_shape=[jax.ShapeD...]
    select_n x16 -> x0, other arithmetic: 19.7 us -> none  [step(): return jnp.where(reached, new, before)]
    dot_general x9 -> x0, matrix products: 7.32 us -> none  [the longest x1 2.08 us: per_device(): jnp.einsum('ric,rij->icj', query_pieces, gradient_pieces, preferred_eleme...]
    unnamed x9 -> x11, local copies, waits for them, and re-layouts: 3.9 us -> 6.17 us
  transfers between devices with their start and end apart: 2 -> 0, of which waited for: 2 -> 0; matrix products, arithmetic and copies ran while one was open for 9% -> 0% of each run, Pallas kernels for 0% -> 0%
where the time goes in v1:
time: 40.9 us; the launch traced here: 40.7 us
  Pallas kernels  33.9 us (83%)
  local copies, waits for them, and re-layouts  6.17 us (15%)
  between operations  0.65 us (2%)
    pallas_call x1, Pallas kernels, per_device(): pl.pallas_call(functools.partial(kernel, n, heads), out_shape=[jax.ShapeD...  33.9 us
    unnamed x11, local copies, waits for them, and re-layouts  6.17 us

profile of v1, /device:TPU:0, one launch (start us, length us, event | category | flops | bytes accessed | tf_op | source)
XLA Modules:
  0.0 40.7 jit_solution(6245080088896233905)
XLA Ops:
  0.6 0.0 copy-start
  0.6 0.9 %copy-done = bf16[128,1024]{1,0:T(8,128)(2,1)S(1)} copy-done((bf16[128,1024]{1,0:T(8,128)(2,1)S(1)}, bf16[128,1024]{1,0:T(8,128)(2,1)}, u32[]{:S(2)}) %copy-start) | copy-done | bytes 262168
  1.6 0.0 copy-start.1
  1.6 0.9 %copy-done.1 = bf16[128,1024]{1,0:T(8,128)(2,1)S(1)} copy-done((bf16[128,1024]{1,0:T(8,128)(2,1)S(1)}, bf16[128,1024]{1,0:T(8,128)(2,1)}, u32[]{:S(2)}) %copy-start.1) | copy-done | bytes 262168
  2.5 0.0 copy-start.2
  2.5 0.9 %copy-done.2 = bf16[128,1024]{1,0:T(8,128)(2,1)S(1)} copy-done((bf16[128,1024]{1,0:T(8,128)(2,1)S(1)}, bf16[128,1024]{1,0:T(8,128)(2,1)}, u32[]{:S(2)}) %copy-start.2) | copy-done | bytes 262168
  3.5 0.0 copy-start.3
  3.5 0.9 %copy-done.3 = bf16[128,1024]{1,0:T(8,128)(2,1)S(1)} copy-done((bf16[128,1024]{1,0:T(8,128)(2,1)S(1)}, bf16[128,1024]{1,0:T(8,128)(2,1)}, u32[]{:S(2)}) %copy-start.3) | copy-done | bytes 262168
  4.4 33.9 %shard_map.67 = (f32[128,1024]{1,0:T(8,128)S(1)}, f32[128,1024]{1,0:T(8,128)S(1)}, f32[128,1024]{1,0:T(8,128)S(1)}) custom-call(bf16[128,1024]{1,0:T(8,128)(2,1)S(1)} %copy-done, bf16[128,1024]{1,0:T(8,128)(2,1)S(1)} %copy-done.1, bf16[128,1024]{1,0:T(8,128)(2,1)S(1)} %copy-done.2, bf16[128,1024]{1,0:T(8,128)(2,1)S(1)} %copy-done.3), custom_call_target="tpu_custom_call" | custom-call | tf_op jit(solution)/shard_map/pallas_call | solution.py:197
  38.3 0.8 %copy.10 = f32[128,1024]{1,0:T(8,128)} copy(f32[128,1024]{1,0:T(8,128)S(1)} %get-tuple-element.6) | data formatting | bytes 1048576
  39.1 0.8 %copy.11 = f32[128,1024]{1,0:T(8,128)} copy(f32[128,1024]{1,0:T(8,128)S(1)} %get-tuple-element.7) | data formatting | bytes 1048576
  39.9 0.8 %copy.12 = f32[128,1024]{1,0:T(8,128)} copy(f32[128,1024]{1,0:T(8,128)S(1)} %get-tuple-element.8) | data formatting | bytes 1048576
Async XLA Ops:
  0.6 1.0 %copy-start = (bf16[128,1024]{1,0:T(8,128)(2,1)S(1)}, bf16[128,1024]{1,0:T(8,128)(2,1)}, u32[]{:S(2)}) copy-start(bf16[128,1024]{1,0:T(8,128)(2,1)} %q_hbm.1) | copy-start | bytes 786436
  1.6 0.9 %copy-start.1 = (bf16[128,1024]{1,0:T(8,128)(2,1)S(1)}, bf16[128,1024]{1,0:T(8,128)(2,1)}, u32[]{:S(2)}) copy-start(bf16[128,1024]{1,0:T(8,128)(2,1)} %k_hbm.1) | copy-start | bytes 786436
  2.5 0.9 %copy-start.2 = (bf16[128,1024]{1,0:T(8,128)(2,1)S(1)}, bf16[128,1024]{1,0:T(8,128)(2,1)}, u32[]{:S(2)}) copy-start(bf16[128,1024]{1,0:T(8,128)(2,1)} %v_hbm.1) | copy-start | bytes 786436
  3.5 0.9 %copy-start.3 = (bf16[128,1024]{1,0:T(8,128)(2,1)S(1)}, bf16[128,1024]{1,0:T(8,128)(2,1)}, u32[]{:S(2)}) copy-start(bf16[128,1024]{1,0:T(8,128)(2,1)} %g_hbm.1) | copy-start | bytes 786436

commit v2 on v1

--- a/solution.py
+++ b/solution.py
@@ -21,9 +21,9 @@
 
 def kernel(
     n, heads,
-    q_hbm, k_hbm, v_hbm, g_hbm, dq_hbm, dk_hbm, dv_hbm,
-    rows, own, partner, carry_in, carry_out, grads,
-    load_sem, store_sem, swap_send, swap_recv, chain_send, chain_recv,
+    q_hbm, k_hbm, v_hbm, g_hbm, dq, dk, dv,
+    rows, own, partner, carry_in, carry_out,
+    load_sem, swap_send, swap_recv, chain_send, chain_recv,
 ):
     tok = rows.shape[1]
     me = lax.axis_index("ctx")
@@ -53,9 +53,6 @@
     @pl.when(row < last)
     def _():
         greet(me + 2)
-
-    peers = 1 + jnp.where(row > 0, 1, 0) + jnp.where(row < last, 1, 0)
-    pl.semaphore_wait(barrier, peers)
 
     for load in loads:
         load.wait()
@@ -91,25 +88,21 @@
     def begin(kind):
         return jnp.where(kind == 0, 0, last)
 
-    def start_swaps(kind):
-        needed = (row != edge(kind)) | (side == kind)
-
+    def make(kind, h):
+        own[kind, h] = dot(rows[2 * kind, :, columns(h)], rows[2 * kind + 1, :, columns(h)], 0, 0)
+
+    def give(kind, h):
+        @pl.when((row != edge(kind)) | (side == kind))
+        def _():
+            swap(kind, h).start()
+
+    def start_swaps(kind, from_head):
         def one(h, _):
-            own[kind, h] = dot(rows[2 * kind, :, columns(h)], rows[2 * kind + 1, :, columns(h)], 0, 0)
-
-            @pl.when(needed)
-            def _():
-                swap(kind, h).start()
-
+            make(kind, h)
+            give(kind, h)
             return 0
 
-        lax.fori_loop(0, heads, one, 0)
-
-    def store(i, h):
-        out = (dq_hbm, dk_hbm, dv_hbm)[i]
-        return pltpu.make_async_copy(
-            grads.at[i, :, columns(h)], out.at[:, columns(h)], store_sem.at[i, h]
-        )
+        lax.fori_loop(from_head, heads, one, 0)
 
     def carry(kind, h):
         takes = (row != edge(kind)) | (side == 1 - kind)
@@ -134,18 +127,19 @@
 
         @pl.when(kind == 0)
         def _():
-            grads[0, :, columns(h)] += dot(rows[3, :, columns(h)], total, 1, 1)
-            store(0, h).start()
+            dq[:, columns(h)] += dot(rows[3, :, columns(h)], total, 1, 1)
 
         @pl.when(kind == 1)
         def _():
-            grads[1, :, columns(h)] += dot(rows[1, :, columns(h)], total, 1, 1)
-            store(1, h).start()
-            grads[2, :, columns(h)] += dot(rows[0, :, columns(h)], total, 1, 0)
-            store(2, h).start()
-
-    start_swaps(early)
-    start_swaps(1 - early)
+            dk[:, columns(h)] += dot(rows[1, :, columns(h)], total, 1, 1)
+            dv[:, columns(h)] += dot(rows[0, :, columns(h)], total, 1, 0)
+
+    make(early, 0)
+    peers = 1 + jnp.where(row > 0, 1, 0) + jnp.where(row < last, 1, 0)
+    pl.semaphore_wait(barrier, peers)
+    give(early, 0)
+    start_swaps(early, 1)
+    start_swaps(1 - early, 0)
 
     down = lax.broadcasted_iota(jnp.int32, (tok, tok), 0)
     across = lax.broadcasted_iota(jnp.int32, (tok, tok), 1)
@@ -155,9 +149,9 @@
         dprob = jnp.where(down >= across, dot(g, v, 1, 1), 0.0).astype(BF16)
         dprob_t = jnp.where(down <= across, dot(v, g, 1, 1), 0.0).astype(BF16)
         scores_t = jnp.where(down <= across, dot(k, q, 1, 1), 0.0).astype(BF16)
-        grads[0, :, columns(h)] = dot(dprob, k, 1, 0)
-        grads[1, :, columns(h)] = dot(dprob_t, q, 1, 0)
-        grads[2, :, columns(h)] = dot(scores_t, g, 1, 0)
+        dq[:, columns(h)] = dot(dprob, k, 1, 0)
+        dk[:, columns(h)] = dot(dprob_t, q, 1, 0)
+        dv[:, columns(h)] = dot(scores_t, g, 1, 0)
         carry(early, h)
         return 0
 
@@ -179,11 +173,20 @@
             def _():
                 chain(kind, h).wait_send()
 
-        for i in range(3):
-            store(i, h).wait()
         return 0
 
     lax.fori_loop(0, heads, drain, 0)
+
+
+def deliver(dq, dk, dv, dq_hbm, dk_hbm, dv_hbm, sems):
+    copies = [
+        pltpu.make_async_copy(src, dst, sems.at[i])
+        for i, (src, dst) in enumerate(((dq, dq_hbm), (dk, dk_hbm), (dv, dv_hbm)))
+    ]
+    for copy in copies:
+        copy.start()
+    for copy in copies:
+        copy.wait()
 
 
 def solution(mesh):
@@ -194,23 +197,29 @@
         heads = width // DH
         states = pltpu.VMEM((2, heads, DH, DH), F32)
         sems = pltpu.SemaphoreType.DMA((2, heads))
-        return pl.pallas_call(
+        results = pl.pallas_call(
             functools.partial(kernel, n, heads),
-            out_shape=[jax.ShapeDtypeStruct((tok, width), F32)] * 3,
-            in_specs=[pl.BlockSpec(memory_space=pl.ANY)] * 4,
-            out_specs=[pl.BlockSpec(memory_space=pl.ANY)] * 3,
+            out_shape=[pltpu.VMEM((tok, width), F32)] * 3,
+            in_specs=[pl.BlockSpec(memory_space=pltpu.HBM)] * 4,
+            out_specs=[pl.BlockSpec(memory_space=pltpu.VMEM)] * 3,
             scratch_shapes=[
                 pltpu.VMEM((4, tok, width), BF16),
                 states, states, states, states,
-                pltpu.VMEM((3, tok, width), F32),
                 pltpu.SemaphoreType.DMA((4,)),
-                pltpu.SemaphoreType.DMA((3, heads)),
                 sems, sems, sems, sems,
             ],
             compiler_params=pltpu.CompilerParams(
-                collective_id=0, has_side_effects=True, vmem_limit_bytes=32 << 20
+                collective_id=0, has_side_effects=True, vmem_limit_bytes=60 << 20
             ),
         )(query_rows, key_rows, value_rows, out_grad)
+        return pl.pallas_call(
+            deliver,
+            out_shape=[jax.ShapeDtypeStruct((tok, width), F32)] * 3,
+            in_specs=[pl.BlockSpec(memory_space=pl.ANY)] * 3,
+            out_specs=[pl.BlockSpec(memory_space=pltpu.HBM)] * 3,
+            scratch_shapes=[pltpu.SemaphoreType.DMA((3,))],
+            compiler_params=pltpu.CompilerParams(vmem_limit_bytes=1 << 20),
+        )(*results)
 
     spec = P("ctx", "head")
     return jax.shard_map(

time: 40.9 us -> 35.3 us (0.86)
  local copies, waits for them, and re-layouts: 6.17 us -> 0 us
  Pallas kernels: 33.9 us -> 34.5 us
    unnamed x11 -> x0, local copies, waits for them, and re-layouts: 6.17 us -> none
    pallas_call x1 -> x2, Pallas kernels: 33.9 us -> 34.5 us  [the longest x1 33.3 us: per_device(): pl.pallas_call(functools.partial(kernel, n, heads), out_shape=[pltpu.VMEM...]
where the time goes in v2:
time: 35.3 us; the launch traced here: 35.1 us
  Pallas kernels  34.5 us (98%)
  between operations  0.64 us (2%)
    pallas_call x1, Pallas kernels, per_device(): pl.pallas_call(functools.partial(kernel, n, heads), out_shape=[pltpu.VMEM...  33.3 us
    pallas_call x1, Pallas kernels, per_device(): pl.pallas_call(deliver, out_shape=[jax.ShapeDtypeStruct((tok, width), F32...  1.17 us

profile of v2, /device:TPU:0, one launch (start us, length us, event | category | flops | bytes accessed | tf_op | source)
XLA Modules:
  0.0 35.1 jit_solution(17972698666457519754)
XLA Ops:
  0.6 33.3 %shard_map.67 = (f32[128,1024]{1,0:T(8,128)S(1)}, f32[128,1024]{1,0:T(8,128)S(1)}, f32[128,1024]{1,0:T(8,128)S(1)}) custom-call(bf16[128,1024]{1,0:T(8,128)(2,1)} %q_hbm.1, bf16[128,1024]{1,0:T(8,128)(2,1)} %k_hbm.1, bf16[128,1024]{1,0:T(8,128)(2,1)} %v_hbm.1, bf16[128,1024]{1,0:T(8,128)(2,1)} %g_hbm.1), custom_call_target="tpu_custom_call" | custom-call | tf_op jit(solution)/shard_map/pallas_call | solution.py:200
  34.0 1.2 %shard_map.68 = (f32[128,1024]{1,0:T(8,128)}, f32[128,1024]{1,0:T(8,128)}, f32[128,1024]{1,0:T(8,128)}) custom-call(f32[128,1024]{1,0:T(8,128)S(1)} %get-tuple-element.6.dq, f32[128,1024]{1,0:T(8,128)S(1)} %get-tuple-element.7.dk, f32[128,1024]{1,0:T(8,128)S(1)} %get-tuple-element.8.dv), custom_call_target="tpu_custom_call" | custom-call | tf_op jit(solution)/shard_map/pallas_call | solution.py:215

commit v3 on v2

--- a/solution.py
+++ b/solution.py
@@ -57,9 +57,9 @@
     for load in loads:
         load.wait()
 
-    def swap(kind, h):
+    def swap(source, kind, h):
         return pltpu.make_async_remote_copy(
-            src_ref=own.at[kind, h],
+            src_ref=source.at[kind, h],
             dst_ref=partner.at[kind, h],
             send_sem=swap_send.at[kind, h],
             recv_sem=swap_recv.at[kind, h],
@@ -82,19 +82,25 @@
 
     early = jnp.where(2 * row <= last, 0, 1)
 
-    def edge(kind):
-        return jnp.where(kind == 0, last, 0)
-
-    def begin(kind):
-        return jnp.where(kind == 0, 0, last)
+    def place(kind):
+        return jnp.where(kind == 0, row, last - row)
+
+    def lean(kind):
+        return side == 1 - kind
+
+    third = 3 * heads // 8
+
+    def skip(h):
+        late = jnp.where(h < third, 2, jnp.where(h < 2 * third, 1, 0))
+        return jnp.maximum(last - late, 0)
 
     def make(kind, h):
         own[kind, h] = dot(rows[2 * kind, :, columns(h)], rows[2 * kind + 1, :, columns(h)], 0, 0)
 
     def give(kind, h):
-        @pl.when((row != edge(kind)) | (side == kind))
-        def _():
-            swap(kind, h).start()
+        @pl.when((side == kind) | (place(kind) < skip(h)))
+        def _():
+            swap(own, kind, h).start()
 
     def start_swaps(kind, from_head):
         def one(h, _):
@@ -105,24 +111,29 @@
         lax.fori_loop(from_head, heads, one, 0)
 
     def carry(kind, h):
-        takes = (row != edge(kind)) | (side == 1 - kind)
-
-        @pl.when(takes)
-        def _():
-            swap(kind, h).wait_recv()
-
-        @pl.when(row != begin(kind))
+        at, stop, thin = place(kind), skip(h), lean(kind)
+        inside = thin | (at <= stop)
+
+        @pl.when((at > 0) & inside)
         def _():
             chain(kind, h).wait_recv()
 
-        before = jnp.where(row != begin(kind), carry_in[kind, h], 0.0)
-
-        @pl.when(row != edge(kind))
+        @pl.when((at > stop) & thin)
+        def _():
+            swap(carry_in, kind, h).start()
+
+        @pl.when((at != stop) | thin)
+        def _():
+            swap(own, kind, h).wait_recv()
+
+        before = jnp.where(inside, jnp.where(at > 0, carry_in[kind, h], 0.0), partner[kind, h])
+
+        @pl.when(jnp.where(thin, at < last, at < stop))
         def _():
             carry_out[kind, h] = before + own[kind, h] + partner[kind, h]
             chain(kind, h).start()
 
-        total = before + jnp.where(side == 1 - kind, partner[kind, h], 0.0)
+        total = before + jnp.where(thin, partner[kind, h], 0.0)
         total = total.astype(BF16)
 
         @pl.when(kind == 0)
@@ -165,11 +176,13 @@
 
     def drain(h, _):
         for kind in range(2):
-            @pl.when((row != edge(kind)) | (side == kind))
+            at, stop, thin = place(kind), skip(h), lean(kind)
+
+            @pl.when((at != stop) | ~thin)
             def _():
-                swap(kind, h).wait_send()
-
-            @pl.when(row != edge(kind))
+                swap(own, kind, h).wait_send()
+
+            @pl.when(jnp.where(thin, at < last, at < stop))
             def _():
                 chain(kind, h).wait_send()
 

time: 35.3 us -> 35.1 us (level)
  no operation moved by 1% of the time
where the time goes in v3:
time: 35.1 us; the launch traced here: 34.8 us
  Pallas kernels  34.2 us (97%)
  between operations  0.64 us (2%)
    pallas_call x1, Pallas kernels, per_device(): pl.pallas_call(functools.partial(kernel, n, heads), out_shape=[pltpu.VMEM...  33 us
    pallas_call x1, Pallas kernels, per_device(): pl.pallas_call(deliver, out_shape=[jax.ShapeDtypeStruct((tok, width), F32...  1.17 us

profile of v3, /device:TPU:0, one launch (start us, length us, event | category | flops | bytes accessed | tf_op | source)
XLA Modules:
  0.0 34.8 jit_solution(15624741953979000590)
XLA Ops:
  0.6 33.0 %shard_map.67 = (f32[128,1024]{1,0:T(8,128)S(1)}, f32[128,1024]{1,0:T(8,128)S(1)}, f32[128,1024]{1,0:T(8,128)S(1)}) custom-call(bf16[128,1024]{1,0:T(8,128)(2,1)} %q_hbm.1, bf16[128,1024]{1,0:T(8,128)(2,1)} %k_hbm.1, bf16[128,1024]{1,0:T(8,128)(2,1)} %v_hbm.1, bf16[128,1024]{1,0:T(8,128)(2,1)} %g_hbm.1), custom_call_target="tpu_custom_call" | custom-call | tf_op jit(solution)/shard_map/pallas_call | solution.py:213
  33.7 1.2 %shard_map.68 = (f32[128,1024]{1,0:T(8,128)}, f32[128,1024]{1,0:T(8,128)}, f32[128,1024]{1,0:T(8,128)}) custom-call(f32[128,1024]{1,0:T(8,128)S(1)} %get-tuple-element.6.dq, f32[128,1024]{1,0:T(8,128)S(1)} %get-tuple-element.7.dk, f32[128,1024]{1,0:T(8,128)S(1)} %get-tuple-element.8.dv), custom_call_target="tpu_custom_call" | custom-call | tf_op jit(solution)/shard_map/pallas_call | solution.py:228

commit v4 on v3

--- a/solution.py
+++ b/solution.py
@@ -8,6 +8,7 @@
 from jax.sharding import PartitionSpec as P
 
 DH = 128
+LAG = 4
 MESH = pl.DeviceIdType.MESH
 F32 = jnp.float32
 BF16 = jnp.bfloat16
@@ -91,8 +92,8 @@
     third = 3 * heads // 8
 
     def skip(h):
-        late = jnp.where(h < third, 2, jnp.where(h < 2 * third, 1, 0))
-        return jnp.maximum(last - late, 0)
+        short = jnp.where(h < third, 2, jnp.where(h < 2 * third, 1, 0))
+        return jnp.maximum(last - short, 0)
 
     def make(kind, h):
         own[kind, h] = dot(rows[2 * kind, :, columns(h)], rows[2 * kind + 1, :, columns(h)], 0, 0)
@@ -155,7 +156,7 @@
     down = lax.broadcasted_iota(jnp.int32, (tok, tok), 0)
     across = lax.broadcasted_iota(jnp.int32, (tok, tok), 1)
 
-    def first(h, _):
+    def in_block(h):
         k, v, q, g = (rows[i, :, columns(h)] for i in range(4))
         dprob = jnp.where(down >= across, dot(g, v, 1, 1), 0.0).astype(BF16)
         dprob_t = jnp.where(down <= across, dot(v, g, 1, 1), 0.0).astype(BF16)
@@ -163,16 +164,24 @@
         dq[:, columns(h)] = dot(dprob, k, 1, 0)
         dk[:, columns(h)] = dot(dprob_t, q, 1, 0)
         dv[:, columns(h)] = dot(scores_t, g, 1, 0)
-        carry(early, h)
+
+    late = 1 - early
+    lag = jnp.where((place(early) == 0) | (side == late), heads, min(LAG, heads))
+    turn = jnp.where(side == late, 2 * third, 0)
+
+    def step(t, _):
+        @pl.when(t < heads)
+        def _():
+            in_block(t)
+            carry(early, t)
+
+        @pl.when((t >= lag) & (t < lag + heads))
+        def _():
+            carry(late, lax.rem(t - lag + turn, heads))
+
         return 0
 
-    lax.fori_loop(0, heads, first, 0)
-
-    def second(h, _):
-        carry(1 - early, h)
-        return 0
-
-    lax.fori_loop(0, heads, second, 0)
+    lax.fori_loop(0, 2 * heads, step, 0)
 
     def drain(h, _):
         for kind in range(2):

time: 35.1 us -> 32.2 us (0.917)
  Pallas kernels: 34.2 us -> 31.4 us
    pallas_call x1, Pallas kernels: 33 us -> 30.2 us  [per_device(): pl.pallas_call(functools.partial(kernel, n, heads), out_shape=[pltpu.VMEM...]
where the time goes in v4:
time: 32.2 us; the launch traced here: 32 us
  Pallas kernels  31.4 us (98%)
  between operations  0.64 us (2%)
    pallas_call x1, Pallas kernels, per_device(): pl.pallas_call(functools.partial(kernel, n, heads), out_shape=[pltpu.VMEM...  30.2 us
    pallas_call x1, Pallas kernels, per_device(): pl.pallas_call(deliver, out_shape=[jax.ShapeDtypeStruct((tok, width), F32...  1.17 us

profile of v4, /device:TPU:0, one launch (start us, length us, event | category | flops | bytes accessed | tf_op | source)
XLA Modules:
  0.0 32.0 jit_solution(3168149773994255693)
XLA Ops:
  0.6 30.2 %shard_map.67 = (f32[128,1024]{1,0:T(8,128)S(1)}, f32[128,1024]{1,0:T(8,128)S(1)}, f32[128,1024]{1,0:T(8,128)S(1)}) custom-call(bf16[128,1024]{1,0:T(8,128)(2,1)} %q_hbm.1, bf16[128,1024]{1,0:T(8,128)(2,1)} %k_hbm.1, bf16[128,1024]{1,0:T(8,128)(2,1)} %v_hbm.1, bf16[128,1024]{1,0:T(8,128)(2,1)} %g_hbm.1), custom_call_target="tpu_custom_call" | custom-call | tf_op jit(solution)/shard_map/pallas_call | solution.py:222
  30.9 1.2 %shard_map.68 = (f32[128,1024]{1,0:T(8,128)}, f32[128,1024]{1,0:T(8,128)}, f32[128,1024]{1,0:T(8,128)}) custom-call(f32[128,1024]{1,0:T(8,128)S(1)} %get-tuple-element.6.dq, f32[128,1024]{1,0:T(8,128)S(1)} %get-tuple-element.7.dk, f32[128,1024]{1,0:T(8,128)S(1)} %get-tuple-element.8.dv), custom_call_target="tpu_custom_call" | custom-call | tf_op jit(solution)/shard_map/pallas_call | solution.py:237

commit v5 on v4

--- a/solution.py
+++ b/solution.py
@@ -8,7 +8,7 @@
 from jax.sharding import PartitionSpec as P
 
 DH = 128
-LAG = 4
+LAG = 3
 MESH = pl.DeviceIdType.MESH
 F32 = jnp.float32
 BF16 = jnp.bfloat16

time: 32.2 us -> 31.4 us (0.975)
  Pallas kernels: 31.4 us -> 30.6 us
    pallas_call x1, Pallas kernels: 30.2 us -> 29.4 us  [per_device(): pl.pallas_call(functools.partial(kernel, n, heads), out_shape=[pltpu.VMEM...]
where the time goes in v5:
time: 31.4 us; the launch traced here: 31.2 us
  Pallas kernels  30.6 us (97%)
  between operations  0.64 us (2%)
    pallas_call x1, Pallas kernels, per_device(): pl.pallas_call(functools.partial(kernel, n, heads), out_shape=[pltpu.VMEM...  29.4 us
    pallas_call x1, Pallas kernels, per_device(): pl.pallas_call(deliver, out_shape=[jax.ShapeDtypeStruct((tok, width), F32...  1.17 us

profile of v5, /device:TPU:0, one launch (start us, length us, event | category | flops | bytes accessed | tf_op | source)
XLA Modules:
  0.0 31.2 jit_solution(5706104867994030257)
XLA Ops:
  0.6 29.4 %shard_map.67 = (f32[128,1024]{1,0:T(8,128)S(1)}, f32[128,1024]{1,0:T(8,128)S(1)}, f32[128,1024]{1,0:T(8,128)S(1)}) custom-call(bf16[128,1024]{1,0:T(8,128)(2,1)} %q_hbm.1, bf16[128,1024]{1,0:T(8,128)(2,1)} %k_hbm.1, bf16[128,1024]{1,0:T(8,128)(2,1)} %v_hbm.1, bf16[128,1024]{1,0:T(8,128)(2,1)} %g_hbm.1), custom_call_target="tpu_custom_call" | custom-call | tf_op jit(solution)/shard_map/pallas_call | solution.py:222
  30.1 1.2 %shard_map.68 = (f32[128,1024]{1,0:T(8,128)}, f32[128,1024]{1,0:T(8,128)}, f32[128,1024]{1,0:T(8,128)}) custom-call(f32[128,1024]{1,0:T(8,128)S(1)} %get-tuple-element.6.dq, f32[128,1024]{1,0:T(8,128)S(1)} %get-tuple-element.7.dk, f32[128,1024]{1,0:T(8,128)S(1)} %get-tuple-element.8.dv), custom_call_target="tpu_custom_call" | custom-call | tf_op jit(solution)/shard_map/pallas_call | solution.py:237

commit v6 on v5

--- a/solution.py
+++ b/solution.py
@@ -37,8 +37,17 @@
         pltpu.make_async_copy(src, rows.at[i], load_sem.at[i])
         for i, src in enumerate((k_hbm, v_hbm, q_hbm, g_hbm))
     ]
-    for load in loads:
-        load.start()
+    early = jnp.where(2 * row <= last, 0, 1)
+
+    def of_kind(kind, act):
+        for k in range(2):
+            @pl.when(kind == k)
+            def _():
+                act(loads[2 * k])
+                act(loads[2 * k + 1])
+
+    of_kind(early, lambda load: load.start())
+    of_kind(1 - early, lambda load: load.start())
 
     barrier = pltpu.get_barrier_semaphore()
 
@@ -55,8 +64,7 @@
     def _():
         greet(me + 2)
 
-    for load in loads:
-        load.wait()
+    of_kind(early, lambda load: load.wait())
 
     def swap(source, kind, h):
         return pltpu.make_async_remote_copy(
@@ -81,7 +89,6 @@
     def columns(h):
         return pl.ds(pl.multiple_of(h * DH, DH), DH)
 
-    early = jnp.where(2 * row <= last, 0, 1)
 
     def place(kind):
         return jnp.where(kind == 0, row, last - row)
@@ -151,6 +158,7 @@
     pl.semaphore_wait(barrier, peers)
     give(early, 0)
     start_swaps(early, 1)
+    of_kind(1 - early, lambda load: load.wait())
     start_swaps(1 - early, 0)
 
     down = lax.broadcasted_iota(jnp.int32, (tok, tok), 0)

time: 31.4 us -> 31.2 us (level)
  no operation moved by 1% of the time
where the time goes in v6:
time: 31.2 us; the launch traced here: 31.1 us
  Pallas kernels  30.4 us (97%)
  between operations  0.64 us (2%)
    pallas_call x1, Pallas kernels, per_device(): pl.pallas_call(functools.partial(kernel, n, heads), out_shape=[pltpu.VMEM...  29.3 us
    pallas_call x1, Pallas kernels, per_device(): pl.pallas_call(deliver, out_shape=[jax.ShapeDtypeStruct((tok, width), F32...  1.17 us

profile of v6, /device:TPU:0, one launch (start us, length us, event | category | flops | bytes accessed | tf_op | source)
XLA Modules:
  0.0 31.1 jit_solution(7130434868115349558)
XLA Ops:
  0.6 29.3 %shard_map.67 = (f32[128,1024]{1,0:T(8,128)S(1)}, f32[128,1024]{1,0:T(8,128)S(1)}, f32[128,1024]{1,0:T(8,128)S(1)}) custom-call(bf16[128,1024]{1,0:T(8,128)(2,1)} %q_hbm.1, bf16[128,1024]{1,0:T(8,128)(2,1)} %k_hbm.1, bf16[128,1024]{1,0:T(8,128)(2,1)} %v_hbm.1, bf16[128,1024]{1,0:T(8,128)(2,1)} %g_hbm.1), custom_call_target="tpu_custom_call" | custom-call | tf_op jit(solution)/shard_map/pallas_call | solution.py:230
  29.9 1.2 %shard_map.68 = (f32[128,1024]{1,0:T(8,128)}, f32[128,1024]{1,0:T(8,128)}, f32[128,1024]{1,0:T(8,128)}) custom-call(f32[128,1024]{1,0:T(8,128)S(1)} %get-tuple-element.6.dq, f32[128,1024]{1,0:T(8,128)S(1)} %get-tuple-element.7.dk, f32[128,1024]{1,0:T(8,128)S(1)} %get-tuple-element.8.dv), custom_call_target="tpu_custom_call" | custom-call | tf_op jit(solution)/shard_map/pallas_call | solution.py:245
